TPU v7x, 256 devices: a whole 4x4x8 slice. The times are simulated.
256 devices in a mesh: row: 4 (over y), col: 32 (over x_lo, z, core), feat: 2 (over x_hi).
Axes of the slice: x: 4 (x_hi: 2, x_lo: 2; x = x_hi * 2 + x_lo), y: 4, z: 8, core: 2. Of those that a mesh axis runs over, the one named last changes fastest.
Arguments:
- panel_student: bfloat16 [2048, 4096], P('row', 'feat'), may hold values from -0.01171875 to 0.01171875
- panel_teacher: bfloat16 [2048, 4096], P('row', 'feat'), may hold values from -0.01171875 to 0.01171875
- tokens_student: bfloat16 [24576, 4096], P('col', 'feat'), may hold values from -0.01171875 to 0.01171875
- tokens_teacher: bfloat16 [24576, 4096], P('col', 'feat'), may hold values from -0.01171875 to 0.01171875
Outputs:
- row_loss: float32 [2048], P(('row', 'col'))
- grad_panel: bfloat16 [2048, 4096], P(('row', 'col'), 'feat')
- grad_tokens: bfloat16 [24576, 4096], P('col', 'feat')
All inputs are finite; a program needn't handle non-finite values.
Results may differ from a plain program's by a relative error of at most 0.0058.
Values may be sent and summed in bfloat16 or wider, within the bound.
No kernel may reach another device: no remote copies, remote signals or barrier semaphores. Data moves between devices by JAX's collectives and lax.ppermute only.
A program may use at most 128 MiB of HBM per device.

v0:
```python
import jax
import jax.numpy as jnp
from jax import lax
from jax.sharding import PartitionSpec as P

epsilon = 1e-06


def squares(features):
    values = features.astype(jnp.float32)
    return jnp.sum(values * values, axis=1)


def inner(left, right):
    return jnp.einsum("rd,cd->rc", left, right, preferred_element_type=jnp.float32)


def inverse(total):
    return 1.0 / jnp.sqrt(total + epsilon)


def local(panel_student, panel_teacher, tokens_student, tokens_teacher):
    student_dots, teacher_dots, sq_ps, sq_pt, sq_ts, sq_tt = lax.psum(
        (
            inner(panel_student, tokens_student),
            inner(panel_teacher, tokens_teacher),
            squares(panel_student),
            squares(panel_teacher),
            squares(tokens_student),
            squares(tokens_teacher),
        ),
        "feat",
    )
    inv_ps = inverse(sq_ps)
    inv_pt = inverse(sq_pt)
    inv_ts = inverse(sq_ts)
    inv_tt = inverse(sq_tt)
    student_gram = student_dots * inv_ps[:, None] * inv_ts[None, :]
    teacher_gram = teacher_dots * inv_pt[:, None] * inv_tt[None, :]
    mismatch = student_gram - teacher_gram
    loss_part = jnp.sum(mismatch * mismatch, axis=1)
    doubled = (2.0 * mismatch).astype(jnp.bfloat16)
    panel_unit = panel_student.astype(jnp.float32) * inv_ps[:, None]
    token_unit = tokens_student.astype(jnp.float32) * inv_ts[:, None]
    panel_half = panel_unit.astype(jnp.bfloat16)
    token_half = token_unit.astype(jnp.bfloat16)
    panel_part = jnp.dot(doubled, token_half, preferred_element_type=jnp.float32)
    panel_term, row_loss = (
        lax.psum_scatter(panel_part, "col", scatter_dimension=0, tiled=True),
        lax.psum_scatter(loss_part, "col", scatter_dimension=0, tiled=True),
    )
    token_part = jnp.einsum("rc,rd->cd", doubled, panel_half, preferred_element_type=jnp.float32)
    token_term = lax.psum(token_part, "row")
    share = panel_student.shape[0] // lax.axis_size("col")
    offset = lax.axis_index("col") * share
    unit_rows = lax.dynamic_slice_in_dim(panel_unit, offset, share, 0)
    inv_rows = lax.dynamic_slice_in_dim(inv_ps, offset, share, 0)
    along_panel, along_tokens = lax.psum(
        (jnp.sum(unit_rows * panel_term, axis=1), jnp.sum(token_unit * token_term, axis=1)), "feat"
    )
    grad_panel = ((panel_term - unit_rows * along_panel[:, None]) * inv_rows[:, None]).astype(
        jnp.bfloat16
    )
    grad_tokens = ((token_term - token_unit * along_tokens[:, None]) * inv_ts[:, None]).astype(
        jnp.bfloat16
    )
    return (row_loss, grad_panel, grad_tokens)


def solution(mesh):
    placed = (P("row", "feat"), P("row", "feat"), P("col", "feat"), P("col", "feat"))
    return jax.shard_map(
        local,
        mesh=mesh,
        in_specs=placed,
        out_specs=(P(("row", "col")), P(("row", "col"), "feat"), P("col", "feat")),
        check_vma=False,
    )
```

profile of v0, /device:TPU:8, one launch (start us, length us, event | category | flops | bytes accessed | tf_op | source)
XLA Modules:
  0.0 405.1 jit_solution(3159031561422616562)
XLA Ops:
  7.2 0.0 copy-start
  7.2 0.0 all-reduce.9.cloned.1.call-start
  7.2 0.0 copy-start.1
  7.2 5.7 %fusion.17 = f32[512,768]{1,0:T(8,128)} fusion(bf16[512,2048]{1,0:T(8,128)(2,1)} %param.5, bf16[768,2048]{1,0:T(8,128)(2,1)} %param.7), kind=kOutput, calls=%fused_computation.31 | convolution fusion | flops 1610612736 | bytes 6815744 | tf_op jit(solution)/shard_map/rd,cd->rc/dot_general | solution.py:15
  12.9 0.0 copy-done
  12.9 0.0 copy-done.1
  12.9 3.1 fusion.16
  15.9 0.0 all-reduce.9.cloned.1.call-update
  16.0 0.0 all-reduce.7.cloned.1.call-start
  16.0 0.0 copy-start.2
  16.0 2.2 multiply_reduce_fusion.1
  18.3 0.0 copy-done.2
  18.3 0.5 fusion.8
  18.7 2.6 multiply_reduce_fusion
  21.3 0.7 fusion.7
  22.0 11.1 %all-reduce.2 = (f32[768]{0:T(1024)S(1)}, f32[512]{0:T(512)S(1)}, f32[768]{0:T(1024)S(1)}, f32[512]{0:T(512)S(1)}) all-reduce(f32[768]{0:T(1024)S(1)} %multiply_reduce_fusion, f32[512]{0:T(512)S(1)} %multiply_reduce_fusion.1, f32[768]{0:T(1024)S(1)} %fusion.7, f32[512]{0:T(512)S(1)} %fusion.8), channel_id=1, replica_groups=mesh['row'=4,'col'=32,'feat'=2] {'feat'}, use_global_device_ids=true, to_apply=%region_9.0 | all-reduce | flops 2560 | bytes 20480 | tf_op jit(solution)/shard_map/psum | solution.py:23
  33.1 85.0 %all-reduce.9.cloned.1.call-done = (f32[512,768]{1,0:T(8,128)}, f32[512,768]{1,0:T(8,128)}) async-done(((f32[512,768]{1,0:T(8,128)}, f32[512,768]{1,0:T(8,128)}), (f32[512,768]{1,0:T(8,128)}, f32[512,768]{1,0:T(8,128)})) %all-reduce.9.cloned.1.call-update) | async-done | bytes 3145744 | tf_op jit(solution)/shard_map/psum | solution.py:23
  118.1 0.0 copy-start.3
  118.1 2.6 multiply_reduce_fusion.2
  120.8 0.0 copy-start.4
  120.8 1.1 copy-done.4
  121.9 0.0 copy-done.3
  121.9 4.6 %fusion.12 = f32[768,2048]{1,0:T(8,128)} fusion(f32[512,768]{1,0:T(8,128)S(1)} %get-tuple-element.12, bf16[512,2048]{1,0:T(8,128)(2,1)S(1)} %copy-done.3, f32[512]{0:T(512)S(1)} %get-tuple-element.16), kind=kOutput, calls=%fused_computation.17 | convolution fusion | flops 1614544896 | bytes 9963520 | tf_op jit(solution)/shard_map/rc,rd->cd/dot_general | solution.py:52
  126.5 0.0 all-reduce.7.cloned.1.call-update
  126.5 0.0 reduce-scatter.2.cloned.1.call-start
  126.6 5.2 %fusion.9 = f32[512,2048]{1,0:T(8,128)} fusion(bf16[768,2048]{1,0:T(8,128)(2,1)S(1)} %copy-done, f32[768]{0:T(1024)S(1)} %get-tuple-element.14, f32[512,768]{1,0:T(8,128)} %copy-done.4), kind=kOutput, calls=%fused_computation.15 | convolution fusion | flops 1616117760 | bytes 8915968 | tf_op jit(solution)/shard_map/dot_general | solution.py:47
  131.8 0.0 copy-start.6
  131.8 0.0 reduce-scatter.2.cloned.1.call-update
  131.9 0.1 dynamic_slice.7
  131.9 0.6 copy-done.6
  132.5 0.6 dynamic-slice
  133.7 4.4 %convert_multiply_fusion.2 = f32[512,2048]{1,0:T(8,128)} fusion(bf16[512,2048]{1,0:T(8,128)(2,1)} %param.4, f32[512]{0:T(512)S(1)} %get-tuple-element.16), kind=kLoop, calls=%fused_computation.11 | loop fusion | flops 2097152 | bytes 6293504 | tf_op jit(solution)/shard_map/mul | solution.py:43
  138.2 55.0 %all-reduce = f32[512]{0:T(512)S(1)} all-reduce(f32[512]{0:T(512)S(1)} %get-tuple-element.11), channel_id=2, replica_groups=mesh['row'=4,'col'=32,'feat'=2] {'col'}, use_global_device_ids=true, to_apply=%region_11.0.clone | all-reduce | flops 512 | bytes 4096
  193.2 0.6 dynamic-slice.1
  193.8 63.3 %all-reduce.7.cloned.1.call-done = f32[768,2048]{1,0:T(8,128)} async-done(((f32[768,2048]{1,0:T(8,128)}), f32[768,2048]{1,0:T(8,128)}) %all-reduce.7.cloned.1.call-update) | async-done | bytes 6291472 | tf_op jit(solution)/shard_map/psum | solution.py:53
  257.1 3.7 fusion.3
  260.9 123.8 %reduce-scatter.2.cloned.1.call-done = f32[16,2048]{1,0:T(8,128)} async-done(((f32[512,2048]{1,0:T(8,128)}), f32[16,2048]{1,0:T(8,128)}) %reduce-scatter.2.cloned.1.call-update) | async-done | bytes 131088 | tf_op jit(solution)/shard_map/reduce_scatter | solution.py:49
  384.7 1.1 multiply_reduce_fusion.3
  385.8 6.5 %all-reduce.1 = (f32[16]{0:T(128)S(1)}, f32[768]{0:T(1024)S(1)}) all-reduce(f32[16]{0:T(128)S(1)} %multiply_reduce_fusion.3, f32[768]{0:T(1024)S(1)} %fusion.3), channel_id=1, replica_groups=mesh['row'=4,'col'=32,'feat'=2] {'feat'}, use_global_device_ids=true, to_apply=%region_14.0 | all-reduce | flops 784 | bytes 6272 | tf_op jit(solution)/shard_map/psum | solution.py:58
  392.3 0.0 copy-start.5
  392.3 4.7 %fusion.6 = bf16[768,2048]{1,0:T(8,128)(2,1)} fusion(f32[768,2048]{1,0:T(8,128)} %all-reduce.7.cloned.1.call-done, bf16[768,2048]{1,0:T(8,128)(2,1)S(1)} %copy-done, f32[768]{0:T(1024)S(1)} %get-tuple-element.4, f32[768]{0:T(1024)S(1)} %get-tuple-element.14), kind=kLoop, calls=%fused_computation.8 | loop fusion | flops 9437184 | bytes 12589056 | tf_op jit(solution)/shard_map/convert_element_type | solution.py:64
  397.0 0.0 copy-done.5
  397.0 1.6 multiply_convert_fusion.3
  (2 shorter events, 0.0 us)
Async XLA Ops:
  7.2 5.7 %copy-start = (bf16[768,2048]{1,0:T(8,128)(2,1)S(1)}, bf16[768,2048]{1,0:T(8,128)(2,1)}, u32[]{:S(2)}) copy-start(bf16[768,2048]{1,0:T(8,128)(2,1)} %param.6) | copy-start | bytes 9437188
  7.2 111.0 %all-reduce.9.cloned.1.call-start = ((), (), s32[]{:S(2)}) async-start(), calls=%async_computation.3 | async-start | bytes 6291456 | tf_op jit(solution)/shard_map/psum | solution.py:23
  7.2 5.7 %copy-start.1 = (bf16[512,2048]{1,0:T(8,128)(2,1)S(1)}, bf16[512,2048]{1,0:T(8,128)(2,1)}, u32[]{:S(2)}) copy-start(bf16[512,2048]{1,0:T(8,128)(2,1)} %param.4) | copy-start | bytes 6291460
  16.0 241.1 %all-reduce.7.cloned.1.call-start = ((), (), s32[]{:S(2)}) async-start(), calls=%async_computation.2 | async-start | bytes 12582912 | tf_op jit(solution)/shard_map/psum | solution.py:53
  16.0 2.2 copy-start.2
  118.1 3.8 copy-start.3
  120.8 1.1 copy-start.4
  126.5 258.1 %reduce-scatter.2.cloned.1.call-start = ((), (), s32[]{:S(2)}) async-start(), calls=%async_computation.1 | async-start | bytes 4325376 | tf_op jit(solution)/shard_map/reduce_scatter | solution.py:49
  131.8 0.7 copy-start.6
  392.3 4.7 %copy-start.5 = (f32[16,2048]{1,0:T(8,128)S(1)}, f32[16,2048]{1,0:T(8,128)}, u32[]{:S(2)}) copy-start(f32[16,2048]{1,0:T(8,128)} %reduce-scatter.2.cloned.1.call-done) | copy-start | bytes 393220
Sparse Core Ops, SparseCore 0:
  16.1 101.9 all-reduce.8
  126.7 130.4 all-reduce.6
  259.7 124.9 reduce-scatter.1
where the time goes:
time: 405 us
  waiting for transfers between devices  272 us (67%)
  blocking collectives  72.6 us (18%)
  other arithmetic  24.2 us (6%)
  matrix products  18.5 us (5%)
  between operations  14.5 us (4%)
    reduce_scatter x1, waiting for transfers between devices, local(): lax.psum_scatter(panel_part, 'col', scatter_dimension=0, tiled=True)  124 us
    psum x1, waiting for transfers between devices, local(): lax.psum((inner(panel_student, tokens_student), inner(panel_teacher, toke...  85 us
    psum x1, waiting for transfers between devices, local(): token_term = lax.psum(token_part, 'row')  63.3 us
    unnamed x1, blocking collectives  55 us
    psum x1, blocking collectives, local(): lax.psum((inner(panel_student, tokens_student), inner(panel_teacher, toke...  11.1 us
    dot_general x2, matrix products, inner(): jnp.einsum('rd,cd->rc', left, right, preferred_element_type=jnp.float32)  8.71 us
  transfers between devices with their start and end apart: 3, of which 3 were waited for; matrix products, arithmetic and copies ran while one was open for 5% of the time, Pallas kernels for 0%

commit v1 on v0

--- a/solution.py
+++ b/solution.py
@@ -4,6 +4,14 @@
 from jax.sharding import PartitionSpec as P
 
 epsilon = 1e-06
+
+
+def doubling_sum(x, axis):
+    size, total = (lax.axis_size(axis), x)
+    for far in [1 << k for k in range(size.bit_length() - 1)]:
+        route = [(i, i ^ far) for i in range(size)]
+        total = total + lax.ppermute(total, axis, route)
+    return total
 
 
 def squares(features):
@@ -50,7 +58,7 @@
         lax.psum_scatter(loss_part, "col", scatter_dimension=0, tiled=True),
     )
     token_part = jnp.einsum("rc,rd->cd", doubled, panel_half, preferred_element_type=jnp.float32)
-    token_term = lax.psum(token_part, "row")
+    token_term = doubling_sum(token_part, "row")
     share = panel_student.shape[0] // lax.axis_size("col")
     offset = lax.axis_index("col") * share
     unit_rows = lax.dynamic_slice_in_dim(panel_unit, offset, share, 0)

time: 405 us -> 438 us (1.081)
  waiting for transfers between devices: 272 us -> 294 us
  other arithmetic: 24.2 us -> 35.5 us
    ppermute x0 -> x2, waiting for transfers between devices: none -> 208 us  [doubling_sum(): total = total + lax.ppermute(total, axis, route)]
    reduce_scatter x1, waiting for transfers between devices: 124 us -> 0.01 us  [local(): lax.psum_scatter(panel_part, 'col', scatter_dimension=0, tiled=True)]
    psum x1 -> x0, waiting for transfers between devices: 63.3 us -> none  [local(): token_term = lax.psum(token_part, 'row')]
    add x0 -> x1, other arithmetic: none -> 9.16 us  [doubling_sum(): total = total + lax.ppermute(total, axis, route)]
    reduce_sum x1, other arithmetic: 3.74 us -> 8.34 us  [local(): jnp.sum(token_unit * token_term, axis=1)]
  transfers between devices with their start and end apart: 3 -> 4, of which waited for: 3 -> 3; matrix products, arithmetic and copies ran while one was open for 5% -> 5% of each run, Pallas kernels for 0% -> 0%
where the time goes in v1:
time: 438 us
  waiting for transfers between devices  294 us (67%)
  blocking collectives  72 us (16%)
  other arithmetic  35.5 us (8%)
  matrix products  17.2 us (4%)
  between operations  14.8 us (3%)
    ppermute x2, waiting for transfers between devices, doubling_sum(): total = total + lax.ppermute(total, axis, route)  208 us
    psum x1, waiting for transfers between devices, local(): lax.psum((inner(panel_student, tokens_student), inner(panel_teacher, toke...  85.9 us
    unnamed x1, blocking collectives  54.4 us
    psum x1, blocking collectives, local(): lax.psum((inner(panel_student, tokens_student), inner(panel_teacher, toke...  11.1 us
    add x1, other arithmetic, doubling_sum(): total = total + lax.ppermute(total, axis, route)  9.16 us
  transfers between devices with their start and end apart: 4, of which 3 were waited for; matrix products, arithmetic and copies ran while one was open for 5% of the time, Pallas kernels for 0%

profile of v1, /device:TPU:8, one launch (start us, length us, event | category | flops | bytes accessed | tf_op | source)
XLA Modules:
  0.0 438.0 jit_solution(1045190888579905947)
XLA Ops:
  7.2 0.0 copy-start.2
  7.2 0.0 all-reduce.6.cloned.1.call-start
  7.2 0.0 copy-start.4
  7.2 5.6 %fusion.16 = f32[512,768]{1,0:T(8,128)} fusion(bf16[512,2048]{1,0:T(8,128)(2,1)} %param.4, bf16[768,2048]{1,0:T(8,128)(2,1)} %param.6), kind=kOutput, calls=%fused_computation.30 | convolution fusion | flops 1610612736 | bytes 6815744 | tf_op jit(solution)/shard_map/rd,cd->rc/dot_general | solution.py:23
  12.9 0.0 copy-done.2
  12.9 0.0 copy-done.4
  12.9 3.1 fusion.17
  15.9 0.0 copy-start
  15.9 0.0 all-reduce.6.cloned.1.call-update
  16.0 0.0 reduce-scatter.2.cloned.1.call-start
  16.0 0.0 copy-start.5
  16.0 2.2 fusion.8
  18.3 0.1 copy-done.5
  18.4 0.0 copy-start.3
  18.4 0.5 multiply_reduce_fusion.1
  18.9 0.2 copy-done
  19.1 0.7 fusion.7
  19.8 0.7 copy-done.3
  20.5 0.7 multiply_reduce_fusion
  21.1 11.1 %all-reduce.2 = (f32[768]{0:T(1024)S(1)}, f32[512]{0:T(512)S(1)}, f32[768]{0:T(1024)S(1)}, f32[512]{0:T(512)S(1)}) all-reduce(f32[768]{0:T(1024)S(1)} %multiply_reduce_fusion, f32[512]{0:T(512)S(1)} %multiply_reduce_fusion.1, f32[768]{0:T(1024)S(1)} %fusion.7, f32[512]{0:T(512)S(1)} %fusion.8), channel_id=1, replica_groups=mesh['row'=4,'col'=32,'feat'=2] {'feat'}, use_global_device_ids=true, to_apply=%region_9.0 | all-reduce | flops 2560 | bytes 20480 | tf_op jit(solution)/shard_map/psum | solution.py:31
  32.3 85.9 %all-reduce.6.cloned.1.call-done = (f32[512,768]{1,0:T(8,128)}, f32[512,768]{1,0:T(8,128)}) async-done(((f32[512,768]{1,0:T(8,128)}, f32[512,768]{1,0:T(8,128)}), (f32[512,768]{1,0:T(8,128)}, f32[512,768]{1,0:T(8,128)})) %all-reduce.6.cloned.1.call-update) | async-done | bytes 3145744 | tf_op jit(solution)/shard_map/psum | solution.py:31
  118.2 0.0 copy-start.1
  118.2 2.6 multiply_reduce_fusion.2
  120.8 0.0 copy-done.1
  120.8 4.6 %fusion.12 = f32[768,2048]{1,0:T(8,128)} fusion(f32[512,768]{1,0:T(8,128)S(1)} %get-tuple-element.14, bf16[512,2048]{1,0:T(8,128)(2,1)S(1)} %copy-done.1, f32[512]{0:T(512)S(1)} %get-tuple-element.18), kind=kOutput, calls=%fused_computation.17 | convolution fusion | flops 1614544896 | bytes 9963520 | tf_op jit(solution)/shard_map/rc,rd->cd/dot_general | solution.py:60
  125.4 0.5 collective-permute-start
  125.9 3.9 fusion.9
  129.8 0.0 reduce-scatter.2.cloned.1.call-update
  129.8 0.0 copy-start.7
  129.8 132.9 %collective-permute-done = f32[768,2048]{1,0:T(8,128)} collective-permute-done((f32[768,2048]{1,0:T(8,128)}, f32[768,2048]{1,0:T(8,128)}, u32[]{:S(2)}, u32[]{:S(2)}) %collective-permute-start) | collective-permute-done | bytes 6291488 | tf_op jit(solution)/shard_map/ppermute | solution.py:13
  262.8 9.2 %add.47 = f32[768,2048]{1,0:T(8,128)} add(f32[768,2048]{1,0:T(8,128)} %fusion.12, f32[768,2048]{1,0:T(8,128)} %collective-permute-done) | non-fusion elementwise | flops 1572864 | bytes 18874368 | tf_op jit(solution)/shard_map/add | solution.py:13
  272.0 2.1 collective-permute-start.1
  274.1 0.1 dynamic_slice.7
  274.1 0.0 copy-done.7
  274.1 0.6 dynamic-slice
  275.4 3.9 convert_multiply_fusion.2
  279.2 54.4 %all-reduce = f32[512]{0:T(512)S(1)} all-reduce(f32[512]{0:T(512)S(1)} %get-tuple-element.13), channel_id=2, replica_groups=mesh['row'=4,'col'=32,'feat'=2] {'col'}, use_global_device_ids=true, to_apply=%region_11.0.clone | all-reduce | flops 512 | bytes 4096
  333.7 0.6 dynamic-slice.1
  334.2 0.0 reduce-scatter.2.cloned.1.call-done
  334.3 1.1 multiply_reduce_fusion.3
  335.3 74.7 %collective-permute-done.1 = f32[768,2048]{1,0:T(8,128)} collective-permute-done((f32[768,2048]{1,0:T(8,128)}, f32[768,2048]{1,0:T(8,128)}, u32[]{:S(2)}, u32[]{:S(2)}) %collective-permute-start.1) | collective-permute-done | bytes 6291488 | tf_op jit(solution)/shard_map/ppermute | solution.py:13
  410.0 8.3 %fusion.3 = (f32[768]{0:T(1024)S(1)}, f32[768,2048]{1,0:T(8,128)}) fusion(bf16[768,2048]{1,0:T(8,128)(2,1)S(1)} %copy-done, f32[768]{0:T(1024)S(1)} %get-tuple-element.16, f32[768,2048]{1,0:T(8,128)} %add.47, f32[768,2048]{1,0:T(8,128)} %collective-permute-done.1), kind=kLoop, calls=%fused_computation.5 | loop fusion | flops 7863552 | bytes 22026240 | tf_op jit(solution)/shard_map/reduce_sum | solution.py:67
  418.3 6.5 %all-reduce.1 = (f32[16]{0:T(128)S(1)}, f32[768]{0:T(1024)S(1)}) all-reduce(f32[16]{0:T(128)S(1)} %multiply_reduce_fusion.3, f32[768]{0:T(1024)S(1)} %get-tuple-element.11), channel_id=1, replica_groups=mesh['row'=4,'col'=32,'feat'=2] {'feat'}, use_global_device_ids=true, to_apply=%region_14.0 | all-reduce | flops 784 | bytes 6272 | tf_op jit(solution)/shard_map/psum | solution.py:66
  424.8 0.0 copy-start.6
  424.8 4.7 %fusion.6 = bf16[768,2048]{1,0:T(8,128)(2,1)} fusion(f32[768,2048]{1,0:T(8,128)} %get-tuple-element.12, bf16[768,2048]{1,0:T(8,128)(2,1)S(1)} %copy-done, f32[768]{0:T(1024)S(1)} %get-tuple-element.4, f32[768]{0:T(1024)S(1)} %get-tuple-element.16), kind=kLoop, calls=%fused_computation.8 | loop fusion | flops 9437184 | bytes 12589056 | tf_op jit(solution)/shard_map/convert_element_type | solution.py:72
  429.5 0.0 copy-done.6
  429.5 1.6 multiply_convert_fusion.3
  (2 shorter events, 0.0 us)
Async XLA Ops:
  7.2 5.7 %copy-start.2 = (bf16[768,2048]{1,0:T(8,128)(2,1)S(1)}, bf16[768,2048]{1,0:T(8,128)(2,1)}, u32[]{:S(2)}) copy-start(bf16[768,2048]{1,0:T(8,128)(2,1)} %param.7) | copy-start | bytes 9437188
  7.2 111.0 %all-reduce.6.cloned.1.call-start = ((), (), s32[]{:S(2)}) async-start(), calls=%async_computation.2 | async-start | bytes 6291456 | tf_op jit(solution)/shard_map/psum | solution.py:31
  7.2 5.7 %copy-start.4 = (bf16[512,2048]{1,0:T(8,128)(2,1)S(1)}, bf16[512,2048]{1,0:T(8,128)(2,1)}, u32[]{:S(2)}) copy-start(bf16[512,2048]{1,0:T(8,128)(2,1)} %param.5) | copy-start | bytes 6291460
  15.9 3.2 copy-start
  16.0 318.3 %reduce-scatter.2.cloned.1.call-start = ((), (), s32[]{:S(2)}) async-start(), calls=%async_computation.1 | async-start | bytes 4325376 | tf_op jit(solution)/shard_map/reduce_scatter | solution.py:57
  16.0 2.4 copy-start.5
  18.4 2.1 copy-start.3
  118.2 2.6 copy-start.1
  125.4 137.4 %collective-permute-start = (f32[768,2048]{1,0:T(8,128)}, f32[768,2048]{1,0:T(8,128)}, u32[]{:S(2)}, u32[]{:S(2)}) collective-permute-start(f32[768,2048]{1,0:T(8,128)} %fusion.12), channel_id=1, source_target_pairs={{0,64},{64,0},{128,192},{192,128},{1,65},{65,1},{129,193},{193,129... | collective-permute-start | bytes 18874376 | tf_op jit(solution)/shard_map/ppermute | solution.py:13
  129.8 144.3 %copy-start.7 = (u32[256]{0:T(256)S(1)}, u32[256]{0:T(256)}, u32[]{:S(2)}) copy-start(u32[256]{0:T(256)} %constant.23) | copy-start | bytes 3076
  272.0 138.0 %collective-permute-start.1 = (f32[768,2048]{1,0:T(8,128)}, f32[768,2048]{1,0:T(8,128)}, u32[]{:S(2)}, u32[]{:S(2)}) collective-permute-start(f32[768,2048]{1,0:T(8,128)} %add.47), channel_id=1, source_target_pairs={{0,128},{64,192},{128,0},{192,64},{1,129},{65,193},{129,1},{193,65... | collective-permute-start | bytes 18874376 | tf_op jit(solution)/shard_map/ppermute | solution.py:13
  424.8 4.7 %copy-start.6 = (f32[16,2048]{1,0:T(8,128)S(1)}, f32[16,2048]{1,0:T(8,128)}, u32[]{:S(2)}) copy-start(f32[16,2048]{1,0:T(8,128)} %reduce-scatter.2.cloned.1.call-done) | copy-start | bytes 393220
Sparse Core Ops, SparseCore 0:
  16.1 102.0 all-reduce.5
  130.0 124.1 reduce-scatter.1
